TPU v7x, 32 devices: a whole 2x2x4 slice. The times are simulated.
32 devices in a mesh: expert: 8 (over y, x, core), dp: 4 (over z).
Axes of the slice: x: 2, y: 2, z: 4, core: 2. Of those that a mesh axis runs over, the one named last changes fastest.
Arguments:
- tokens: bfloat16 [4096, 2048], P(('expert', 'dp')), may hold values from -6 to 6
- out_grad: bfloat16 [4096, 2048], P(('expert', 'dp')), may hold values from -1.25 to 1.25
- expert_ids: int32 [4096, 8], P(('expert', 'dp')), may hold values from 0 to 15, all different within a row; in each aligned block of 128 rows (0 to 127, 128 to 255, ...) at most 72 rows name the same one
- route_weight: bfloat16 [4096, 8], P(('expert', 'dp')), may hold values from 0.099609375 to 1
- w_gate_up: bfloat16 [16, 2048, 768], P('expert'), may hold values from -0.125 to 0.125
- w_down: bfloat16 [16, 384, 2048], P('expert'), may hold values from -0.3125 to 0.3125
Outputs:
- d_tokens: bfloat16 [4096, 2048], P(('expert', 'dp'))
- d_route: bfloat16 [4096, 8], P(('expert', 'dp'))
- grad_gate_up: bfloat16 [16, 2048, 768], P('expert', 'dp')
- grad_down: bfloat16 [16, 384, 2048], P('expert', None, 'dp')
Inputs may be any that keep to these rules, and one draw needn't show every extreme that they name: `expert_ids`: each row names 8 different experts. Among the 128 rows of one device (aligned blocks of 128 rows) no expert is named more than 72 times, and in every draw some expert is named exactly 72 times by the rows of some device.
All inputs are finite; a program needn't handle non-finite values.
Results may differ from a plain program's by a relative error of at most 0.012.
Values may be sent and summed in bfloat16 or wider, within the bound.
A program may use at most 128 MiB of HBM per device.

v0:
```python
import jax
import jax.numpy as jnp
from jax import lax
from jax.sharding import PartitionSpec as P


def expert_backward(rows_in, rows_grad, weight, gate_up, down):
    pre_act = jnp.dot(rows_in, gate_up, preferred_element_type=jnp.float32)
    half_width = pre_act.shape[1] // 2
    gate_pre = pre_act[:, :half_width]
    up_pre = pre_act[:, half_width:]
    sigmoid_gate = jax.nn.sigmoid(gate_pre)
    active = gate_pre * sigmoid_gate
    hidden = (active * up_pre).astype(jnp.bfloat16)
    back_hidden = lax.dot_general(
        rows_grad, down, (((1,), (1,)), ((), ())), preferred_element_type=jnp.float32
    )
    route_grad = jnp.sum(back_hidden * hidden.astype(jnp.float32), axis=1).astype(jnp.bfloat16)
    weight_col = weight.astype(jnp.float32)[:, None]
    scaled = weight_col * back_hidden
    grad_gate = scaled * up_pre * sigmoid_gate * (1.0 + gate_pre * (1.0 - sigmoid_gate))
    grad_up = scaled * active
    grad_pre = jnp.concatenate([grad_gate, grad_up], axis=1).astype(jnp.bfloat16)
    route_input = lax.dot_general(
        grad_pre, gate_up, (((1,), (1,)), ((), ())), preferred_element_type=jnp.float32
    ).astype(jnp.bfloat16)
    scaled_hidden = (weight_col * hidden.astype(jnp.float32)).astype(jnp.bfloat16)
    return (route_input, route_grad, grad_pre, scaled_hidden)


def weight_terms(rows_in, rows_grad, grad_pre, scaled_hidden):
    term_gate_up = lax.dot_general(
        rows_in, grad_pre, (((0,), (0,)), ((), ())), preferred_element_type=jnp.float32
    )
    term_down = lax.dot_general(
        scaled_hidden, rows_grad, (((0,), (0,)), ((), ())), preferred_element_type=jnp.float32
    )
    return (term_gate_up, term_down)


def run_expert(arrived_in, arrived_grad, arrived_weight, gate_up, down):
    groups = arrived_in.shape[0]
    capacity = arrived_in.shape[1]
    dim_model = arrived_in.shape[2]
    rows_in = arrived_in.reshape(groups * capacity, dim_model)
    rows_grad = arrived_grad.reshape(groups * capacity, dim_model)
    weight = arrived_weight.reshape(groups * capacity)
    route_input, route_grad, grad_pre, scaled_hidden = expert_backward(
        rows_in, rows_grad, weight, gate_up, down
    )
    shaped_input = route_input.reshape(groups, capacity, dim_model)
    shaped_grad = route_grad.reshape(groups, capacity)
    return (shaped_input, shaped_grad, (rows_in, rows_grad, grad_pre, scaled_hidden))


def slot_numbers(route_experts, all_experts):
    route_count = route_experts.shape[0]
    block_len = 128
    block_count = route_count // block_len
    onehot = (route_experts[:, None] == jnp.arange(all_experts, dtype=jnp.int32)[None, :]).astype(
        jnp.bfloat16
    )
    onehot = onehot.reshape(block_count, block_len, all_experts)
    lower = (jnp.arange(block_len)[:, None] > jnp.arange(block_len)[None, :]).astype(jnp.bfloat16)
    within = jnp.einsum("ij,bje->bie", lower, onehot, preferred_element_type=jnp.float32)
    totals = jnp.sum(onehot.astype(jnp.float32), axis=1)
    earlier = (jnp.arange(block_count)[:, None] > jnp.arange(block_count)[None, :]).astype(
        jnp.float32
    )
    before = jnp.dot(earlier, totals, precision=lax.Precision.HIGHEST)
    counted = jnp.sum((within + before[:, None, :]) * onehot.astype(jnp.float32), axis=2)
    return counted.reshape(route_count).astype(jnp.int32)


def local(tokens, out_grad, expert_ids, route_weight, w_gate_up, w_down):
    tok_rows = tokens.shape[0]
    dim_model = tokens.shape[1]
    top_count = expert_ids.shape[1]
    exp_local = w_gate_up.shape[0]
    groups = lax.axis_size("expert")
    all_experts = exp_local * groups
    route_count = tok_rows * top_count
    capacity = 9 * tok_rows * top_count // (8 * all_experts)
    route_experts = expert_ids.reshape(route_count)
    slot_index = slot_numbers(route_experts, all_experts)
    target = route_experts // exp_local
    local_expert = route_experts % exp_local
    position = local_expert * (groups * capacity) + target * capacity + slot_index
    source_table = jnp.full((all_experts * capacity,), route_count, jnp.int32)
    source_table = source_table.at[position].set(jnp.arange(route_count, dtype=jnp.int32))
    token_of = source_table // top_count
    send_in = jnp.take(tokens, token_of, axis=0, mode="fill", fill_value=0).reshape(
        exp_local, groups, capacity, dim_model
    )
    send_grad = jnp.take(out_grad, token_of, axis=0, mode="fill", fill_value=0).reshape(
        exp_local, groups, capacity, dim_model
    )
    send_weight = jnp.take(
        route_weight.reshape(route_count), source_table, axis=0, mode="fill", fill_value=0
    ).reshape(exp_local, groups, capacity)
    gate_up_terms = []
    down_terms = []
    arrived_in, arrived_grad, arrived_weight = (
        lax.all_to_all(send_in, "expert", split_axis=1, concat_axis=1, tiled=True),
        lax.all_to_all(send_grad, "expert", split_axis=1, concat_axis=1, tiled=True),
        lax.all_to_all(send_weight, "expert", split_axis=1, concat_axis=1, tiled=True),
    )
    inputs_list = []
    grads_list = []
    saved = []
    for which in range(exp_local):
        shaped_input, shaped_grad, kept = run_expert(
            arrived_in[which],
            arrived_grad[which],
            arrived_weight[which],
            w_gate_up[which],
            w_down[which],
        )
        inputs_list.append(shaped_input)
        grads_list.append(shaped_grad)
        saved.append(kept)
    returned_in, returned_route = (
        lax.all_to_all(jnp.stack(inputs_list), "expert", split_axis=1, concat_axis=1, tiled=True),
        lax.all_to_all(jnp.stack(grads_list), "expert", split_axis=1, concat_axis=1, tiled=True),
    )
    for which in range(exp_local):
        term_gate_up, term_down = weight_terms(*saved[which])
        gate_up_terms.append(term_gate_up)
        down_terms.append(term_down)
    summed_gate_up, summed_down = (
        lax.psum_scatter(
            jnp.stack(gate_up_terms).astype(jnp.bfloat16), "dp", scatter_dimension=1, tiled=True
        ).astype(jnp.float32),
        lax.psum_scatter(
            jnp.stack(down_terms).astype(jnp.bfloat16), "dp", scatter_dimension=2, tiled=True
        ).astype(jnp.float32),
    )
    mean_factor = 1.0 / lax.axis_size("dp")
    grad_gate_up = (summed_gate_up * mean_factor).astype(jnp.bfloat16)
    grad_down = (summed_down * mean_factor).astype(jnp.bfloat16)
    back_flat = returned_in.reshape(all_experts * capacity, dim_model)
    route_flat = returned_route.reshape(all_experts * capacity)
    route_rows = jnp.take(back_flat, position, axis=0).reshape(tok_rows, top_count, dim_model)
    d_tokens = jnp.sum(route_rows.astype(jnp.float32), axis=1).astype(jnp.bfloat16)
    d_route = jnp.take(route_flat, position, axis=0).reshape(tok_rows, top_count)
    return (d_tokens, d_route, grad_gate_up, grad_down)


def solution(mesh):
    placed = (
        P(("expert", "dp"), None),
        P(("expert", "dp"), None),
        P(("expert", "dp"), None),
        P(("expert", "dp"), None),
        P("expert", None, None),
        P("expert", None, None),
    )
    return jax.shard_map(
        local,
        mesh=mesh,
        in_specs=placed,
        out_specs=(
            P(("expert", "dp"), None),
            P(("expert", "dp"), None),
            P("expert", "dp", None),
            P("expert", None, "dp"),
        ),
        check_vma=False,
    )
```

profile of v0, /device:TPU:0, one launch (start us, length us, event | category | flops | bytes accessed | tf_op | source)
XLA Modules:
  0.0 364.6 jit_solution(9369899892041569120)
XLA Ops:
  7.2 0.8 copy.32
  8.7 4.3 %scatter_custom_fusion = s32[1152]{0:T(1024)S(1)} fusion(s32[1024]{0:T(1024)S(1)} %bitcast.83, s32[1024]{0:T(1024)S(1)} %iota.30, s32[]{:T(128)} %constant.102.clone.1), kind=kCustom, calls=%fused_computation.119 | custom fusion | bytes 4612 | tf_op jit(solution)/shard_map/scatter | solution.py:90
  13.0 0.8 copy.38
  13.9 7.3 %gather_fusion = bf16[1152]{0:T(1024)(128)(2,1)S(1)} fusion(bf16[1024]{0:T(1024)(128)(2,1)S(1)} %reshape.244, s32[2048]{0:T(1024)S(1)} %pad_clamp_fusion.1), kind=kCustom, calls=%fused_computation.2 | custom fusion | bytes 9216 | tf_op jit(solution)/shard_map/jit(_take)/gather | solution.py:98
  21.3 0.6 copy.39
  21.9 5.2 %all-to-all-start = ((bf16[2,8,72]{2,0,1:T(2,128)(2,1)}), bf16[2,8,72]{2,0,1:T(2,128)(2,1)S(1)}, u32[]{:S(2)}, u32[]{:S(2)}) async-start(bf16[2,8,72]{2,0,1:T(2,128)(2,1)} %copy.39), calls=%async_computation | async-start | bytes 8192 | tf_op jit(solution)/shard_map/all_to_all | solution.py:106
  27.2 5.9 %gather_fusion.3 = bf16[1152,2048]{1,0:T(8,128)(2,1)} fusion(bf16[128,2048]{1,0:T(8,128)(2,1)S(1)} %copy-done, s32[2048]{0:T(1024)S(1)} %pad_clamp_fusion), kind=kCustom, calls=%fused_computation.clone | custom fusion | bytes 9441792 | tf_op jit(solution)/shard_map/jit(_take)/gather | solution.py:95
  33.1 5.9 %gather_fusion.4 = bf16[1152,2048]{1,0:T(8,128)(2,1)} fusion(bf16[128,2048]{1,0:T(8,128)(2,1)S(1)} %copy-done.2, s32[2048]{0:T(1024)S(1)} %pad_clamp_fusion), kind=kCustom, calls=%fused_computation.1.clone | custom fusion | bytes 9441792 | tf_op jit(solution)/shard_map/jit(_take)/gather | solution.py:92
  39.0 5.7 %broadcast_select_fusion = (bf16[1152,2048]{1,0:T(8,128)(2,1)S(1)}, bf16[1152,2048]{1,0:T(8,128)(2,1)}) fusion(bf16[1152,2048]{1,0:T(8,128)(2,1)} %gather_fusion.4, pred[1152]{0:T(1024)(128)(4,1)S(1)} %get-tuple-element.25, bf16[1152,2048]{1,0:T(8,128)(2,1)} %gather_fusion.3), kind=kLoop, calls=%fused_computation.8 | loop fusion | flops 4718592 | bytes 18875520 | tf_op jit(solution)/shard_map/jit(_take)/select_n | solution.py:92
  44.7 2.6 copy.41
  47.3 4.6 %all-to-all-start.2 = ((bf16[2,8,72,2048]{3,2,0,1:T(8,128)(2,1)}), bf16[2,8,72,2048]{3,2,0,1:T(8,128)(2,1)}, u32[]{:S(2)}, u32[]{:S(2)}) async-start(bf16[2,8,72,2048]{3,2,0,1:T(8,128)(2,1)} %copy.41), calls=%async_computation.2 | async-start | bytes 9437184 | tf_op jit(solution)/shard_map/all_to_all | solution.py:104
  51.9 5.2 %copy.40 = bf16[2,8,72,2048]{3,2,0,1:T(8,128)(2,1)} copy(bf16[2,8,72,2048]{3,2,1,0:T(8,128)(2,1)} %bitcast.70) | data formatting | bytes 9437184 | tf_op jit(solution)/shard_map/reshape | solution.py:95
  57.1 49.6 %all-to-all-done.2 = bf16[2,8,72,2048]{3,2,0,1:T(8,128)(2,1)} async-done(((bf16[2,8,72,2048]{3,2,0,1:T(8,128)(2,1)}), bf16[2,8,72,2048]{3,2,0,1:T(8,128)(2,1)}, u32[]{:S(2)}, u32[]{:S(2)}) %all-to-all-start.2) | async-done | bytes 4718624 | tf_op jit(solution)/shard_map/all_to_all | solution.py:104
  106.6 4.6 %all-to-all-start.1 = ((bf16[2,8,72,2048]{3,2,0,1:T(8,128)(2,1)}), bf16[2,8,72,2048]{3,2,0,1:T(8,128)(2,1)}, u32[]{:S(2)}, u32[]{:S(2)}) async-start(bf16[2,8,72,2048]{3,2,0,1:T(8,128)(2,1)} %copy.40), calls=%async_computation.1 | async-start | bytes 9437184 | tf_op jit(solution)/shard_map/all_to_all | solution.py:105
  111.2 0.2 reduce-scatter.5.cloned.1.call-start
  111.7 2.8 fusion.68
  114.4 1.4 copy-done.3
  115.8 5.2 %fusion.7 = f32[576,768]{1,0:T(8,128)} fusion(bf16[576,2048]{1,0:T(8,128)(2,1)S(1)} %bitcast.78, bf16[2,2048,768]{2,1,0:T(8,128)(2,1)} %param.12), kind=kOutput, calls=%fused_computation.21 | convolution fusion | flops 1811939328 | bytes 7274496 | tf_op jit(solution)/shard_map/dot_general | solution.py:8
  121.0 45.0 %all-to-all-done.1 = bf16[2,8,72,2048]{3,2,0,1:T(8,128)(2,1)} async-done(((bf16[2,8,72,2048]{3,2,0,1:T(8,128)(2,1)}), bf16[2,8,72,2048]{3,2,0,1:T(8,128)(2,1)}, u32[]{:S(2)}, u32[]{:S(2)}) %all-to-all-start.1) | async-done | bytes 4718624 | tf_op jit(solution)/shard_map/all_to_all | solution.py:105
  166.0 2.9 fusion.69
  168.9 0.4 copy-done.4
  169.3 0.5 copy-done.5
  169.8 2.5 fusion.32
  172.3 1.5 fusion.21
  173.9 2.0 fusion.3
  175.9 2.7 fusion.34
  178.6 1.5 fusion.22
  180.1 1.9 pad_maximum_fusion.2
  182.1 0.3 reduce-scatter.3.cloned.1.call-start
  182.3 0.7 copy-done.6
  183.1 4.4 %fusion.15 = bf16[1,2048,768]{2,1,0:T(8,128)(2,1)S(1)} fusion(bf16[576,2048]{1,0:T(8,128)(2,1)} %bitcast.79, bf16[576,384]{1,0:T(8,128)(2,1)S(1)} %get-tuple-element.35, bf16[576,384]{1,0:T(8,128)(2,1)S(1)} %copy-done.6), kind=kOutput, calls=%fused_computation.26 | convolution fusion | flops 1815281664 | bytes 6389760 | tf_op jit(solution)/shard_map/dot_general | solution.py:32
  187.5 2.9 fusion.16
  190.4 3.2 pad_maximum_fusion
  193.8 0.6 copy.45
  194.4 3.2 all-to-all-start.4
  197.7 4.2 %fusion.9 = bf16[576,2048]{1,0:T(8,128)(2,1)S(1)} fusion(bf16[2,2048,768]{2,1,0:T(8,128)(2,1)} %param.12, bf16[576,384]{1,0:T(8,128)(2,1)S(1)} %get-tuple-element.35, bf16[576,384]{1,0:T(8,128)(2,1)} %get-tuple-element.36), kind=kOutput, calls=%fused_computation.24 | convolution fusion | flops 1814888448 | bytes 6389760 | tf_op jit(solution)/shard_map/dot_general | solution.py:24
  202.0 2.0 fusion.12
  204.1 2.6 pad_maximum_fusion.1
  206.7 4.9 %all-to-all-start.3 = ((bf16[2,8,72,2048]{3,2,0,1:T(8,128)(2,1)}), bf16[2,8,72,2048]{3,2,0,1:T(8,128)(2,1)}, u32[]{:S(2)}, u32[]{:S(2)}) async-start(bf16[2,8,72,2048]{3,2,0,1:T(8,128)(2,1)} %pad_maximum_fusion.1), calls=%async_computation.3 | async-start | bytes 9437184 | tf_op jit(solution)/shard_map/all_to_all | solution.py:123
  211.8 6.8 %gather_fusion.2 = bf16[1024]{0:T(1024)(128)(2,1)S(1)} fusion(bf16[1152]{0:T(1024)(128)(2,1)S(1)} %reshape.248, s32[1024]{0:T(1024)S(1)} %broadcast_clamp_fusion), kind=kCustom, calls=%fused_computation.4 | custom fusion | bytes 8192 | tf_op jit(solution)/shard_map/jit(_take)/gather | solution.py:145
  218.8 0.7 copy.47
  219.5 46.8 %all-to-all-done.3 = bf16[2,8,72,2048]{3,2,0,1:T(8,128)(2,1)} async-done(((bf16[2,8,72,2048]{3,2,0,1:T(8,128)(2,1)}), bf16[2,8,72,2048]{3,2,0,1:T(8,128)(2,1)}, u32[]{:S(2)}, u32[]{:S(2)}) %all-to-all-start.3) | async-done | bytes 4718624 | tf_op jit(solution)/shard_map/all_to_all | solution.py:123
  266.3 5.3 %copy.44 = bf16[2,8,72,2048]{3,2,1,0:T(8,128)(2,1)} copy(bf16[2,8,72,2048]{3,2,0,1:T(8,128)(2,1)} %all-to-all-done.3) | data formatting | bytes 9437184 | tf_op jit(solution)/shard_map/all_to_all | solution.py:123
  271.5 11.8 %gather_fusion.1 = bf16[1024,2048]{1,0:T(8,128)(2,1)} fusion(bf16[1152,2048]{1,0:T(8,128)(2,1)} %bitcast.69, s32[1024]{0:T(1024)S(1)} %broadcast_clamp_fusion), kind=kCustom, calls=%fused_computation.3 | custom fusion | bytes 8392704 | tf_op jit(solution)/shard_map/jit(_take)/gather | solution.py:143
  283.3 5.2 %fusion = bf16[128,2048]{1,0:T(8,128)(2,1)} fusion(bf16[1024,2048]{1,0:T(8,128)(2,1)} %gather_fusion.1, pred[128,8]{1,0:T(8,128)(4,1)S(1)} %get-tuple-element.20), kind=kLoop, calls=%fused_computation.11 | loop fusion | flops 3932160 | bytes 4719616 | tf_op jit(solution)/shard_map/reduce_sum | solution.py:144
  288.5 2.2 multiply_convert_fusion.1
  290.6 64.3 %reduce-scatter.3.cloned.1.call-done = bf16[2,512,768]{2,1,0:T(8,128)(2,1)} async-done(((bf16[2,2048,768]{2,1,0:T(8,128)(2,1)}), bf16[2,512,768]{2,1,0:T(8,128)(2,1)}) %reduce-scatter.3.cloned.1.call-update) | async-done | bytes 1572880 | tf_op jit(solution)/shard_map/reduce_scatter | solution.py:131
  355.0 2.8 multiply_convert_fusion
  (60 shorter events, 1.7 us)
Async XLA Ops:
  7.2 20.0 %copy-start = (bf16[128,2048]{1,0:T(8,128)(2,1)S(1)}, bf16[128,2048]{1,0:T(8,128)(2,1)}, u32[]{:S(2)}) copy-start(bf16[128,2048]{1,0:T(8,128)(2,1)} %param.9) | copy-start | bytes 1572868
  21.9 25.3 %all-to-all-start = ((bf16[2,8,72]{2,0,1:T(2,128)(2,1)}), bf16[2,8,72]{2,0,1:T(2,128)(2,1)S(1)}, u32[]{:S(2)}, u32[]{:S(2)}) async-start(bf16[2,8,72]{2,0,1:T(2,128)(2,1)} %copy.39), calls=%async_computation | async-start | bytes 8192 | tf_op jit(solution)/shard_map/all_to_all | solution.py:106
  27.2 5.9 %copy-start.2 = (bf16[128,2048]{1,0:T(8,128)(2,1)S(1)}, bf16[128,2048]{1,0:T(8,128)(2,1)}, u32[]{:S(2)}) copy-start(bf16[128,2048]{1,0:T(8,128)(2,1)} %param.8) | copy-start | bytes 1572868
  47.3 59.4 %all-to-all-start.2 = ((bf16[2,8,72,2048]{3,2,0,1:T(8,128)(2,1)}), bf16[2,8,72,2048]{3,2,0,1:T(8,128)(2,1)}, u32[]{:S(2)}, u32[]{:S(2)}) async-start(bf16[2,8,72,2048]{3,2,0,1:T(8,128)(2,1)} %copy.41), calls=%async_computation.2 | async-start | bytes 9437184 | tf_op jit(solution)/shard_map/all_to_all | solution.py:104
  106.6 59.4 %all-to-all-start.1 = ((bf16[2,8,72,2048]{3,2,0,1:T(8,128)(2,1)}), bf16[2,8,72,2048]{3,2,0,1:T(8,128)(2,1)}, u32[]{:S(2)}, u32[]{:S(2)}) async-start(bf16[2,8,72,2048]{3,2,0,1:T(8,128)(2,1)} %copy.40), calls=%async_computation.1 | async-start | bytes 9437184 | tf_op jit(solution)/shard_map/all_to_all | solution.py:105
  111.2 177.3 %reduce-scatter.5.cloned.1.call-start = ((), (), s32[]{:S(2)}) async-start(), calls=%async_computation.8 | async-start | bytes 3932160 | tf_op jit(solution)/shard_map/reduce_scatter | solution.py:134
  114.4 1.4 copy-start.3
  166.0 3.3 copy-start.4
  166.0 3.8 %copy-start.5 = (f32[576,768]{1,0:T(8,128)S(1)}, f32[576,768]{1,0:T(8,128)}, u32[]{:S(2)}) copy-start(f32[576,768]{1,0:T(8,128)} %fusion.7) | copy-start | bytes 5308420
  166.0 7.9 %slice-start = ((s8[6291456]{0:T(1024)(128)(4,1)}), s8[4194304]{0:T(1024)(128)(4,1)S(1)}, s32[]{:S(2)}) async-start(s8[6291456]{0:T(1024)(128)(4,1)} %bitcast.85), calls=%async_computation.9 | async-start | bytes 8388608
  169.8 4.0 %slice-start.1 = ((s8[6291456]{0:T(1024)(128)(4,1)}), s8[2097152]{0:T(1024)(128)(4,1)S(1)}, s32[]{:S(2)}) async-start(s8[6291456]{0:T(1024)(128)(4,1)} %bitcast.85), calls=%async_computation.10 | async-start | bytes 4194304
  182.0 1.0 copy-start.6
  182.1 172.9 %reduce-scatter.3.cloned.1.call-start = ((), (), s32[]{:S(2)}) async-start(), calls=%async_computation.7 | async-start | bytes 7864320 | tf_op jit(solution)/shard_map/reduce_scatter | solution.py:131
  183.0 4.4 %copy-start.7 = (bf16[576,384]{1,0:T(8,128)(2,1)S(1)}, bf16[576,384]{1,0:T(8,128)(2,1)}, u32[]{:S(2)}) copy-start(bf16[576,384]{1,0:T(8,128)(2,1)} %get-tuple-element.37) | copy-start | bytes 1327108
  183.0 4.4 %copy-start.9 = (bf16[576,384]{1,0:T(8,128)(2,1)S(1)}, bf16[576,384]{1,0:T(8,128)(2,1)}, u32[]{:S(2)}) copy-start(bf16[576,384]{1,0:T(8,128)(2,1)} %get-tuple-element.38) | copy-start | bytes 1327108
  193.6 8.4 %slice-start.2 = ((s8[6291456]{0:T(1024)(128)(4,1)}), s8[2097152]{0:T(1024)(128)(4,1)S(1)}, s32[]{:S(2)}) async-start(s8[6291456]{0:T(1024)(128)(4,1)} %bitcast.87), calls=%async_computation.11 | async-start | bytes 4194304
  194.4 12.3 %all-to-all-start.4 = ((bf16[2,8,72]{2,0,1:T(2,128)(2,1)}), bf16[2,8,72]{2,0,1:T(2,128)(2,1)S(1)}, u32[]{:S(2)}, u32[]{:S(2)}) async-start(bf16[2,8,72]{2,0,1:T(2,128)(2,1)} %copy.45), calls=%async_computation.4 | async-start | bytes 8192 | tf_op jit(solution)/shard_map/all_to_all | solution.py:124
  197.7 4.3 %slice-start.3 = ((s8[6291456]{0:T(1024)(128)(4,1)}), s8[4194304]{0:T(1024)(128)(4,1)S(1)}, s32[]{:S(2)}) async-start(s8[6291456]{0:T(1024)(128)(4,1)} %bitcast.87), calls=%async_computation.12 | async-start | bytes 8388608
  197.7 4.3 %copy-start.8 = (bf16[576,384]{1,0:T(8,128)(2,1)S(1)}, bf16[576,384]{1,0:T(8,128)(2,1)}, u32[]{:S(2)}) copy-start(bf16[576,384]{1,0:T(8,128)(2,1)} %get-tuple-element.37) | copy-start | bytes 1327108
  197.7 4.3 %copy-start.10 = (bf16[576,384]{1,0:T(8,128)(2,1)S(1)}, bf16[576,384]{1,0:T(8,128)(2,1)}, u32[]{:S(2)}) copy-start(bf16[576,384]{1,0:T(8,128)(2,1)} %get-tuple-element.38) | copy-start | bytes 1327108
  206.7 59.6 %all-to-all-start.3 = ((bf16[2,8,72,2048]{3,2,0,1:T(8,128)(2,1)}), bf16[2,8,72,2048]{3,2,0,1:T(8,128)(2,1)}, u32[]{:S(2)}, u32[]{:S(2)}) async-start(bf16[2,8,72,2048]{3,2,0,1:T(8,128)(2,1)} %pad_maximum_fusion.1), calls=%async_computation.3 | async-start | bytes 9437184 | tf_op jit(solution)/shard_map/all_to_all | solution.py:123
  283.3 74.5 %copy-start.1 = (bf16[128,2048]{1,0:T(8,128)(2,1)S(1)}, bf16[128,2048]{1,0:T(8,128)(2,1)}, u32[]{:S(2)}) copy-start(bf16[128,2048]{1,0:T(8,128)(2,1)} %param.9) | copy-start | bytes 1572868
Sparse Core Ops, SparseCore 0:
  182.2 59.6 reduce-scatter.4
  244.2 110.7 reduce-scatter.2
where the time goes:
time: 365 us
  waiting for transfers between devices  206 us (56%)
  local copies, waits for them, and re-layouts  68.2 us (19%)
  matrix products  29.4 us (8%)
  other arithmetic  24 us (7%)
  starting transfers between devices  23 us (6%)
  between operations  14.4 us (4%)
    reduce_scatter x1, waiting for transfers between devices, local(): lax.psum_scatter(jnp.stack(gate_up_terms).astype(jnp.bfloat16), 'dp', sca...  64.3 us
    all_to_all x1, waiting for transfers between devices, local(): lax.all_to_all(send_in, 'expert', split_axis=1, concat_axis=1, tiled=True)  49.6 us
    all_to_all x1, waiting for transfers between devices, local(): lax.all_to_all(jnp.stack(inputs_list), 'expert', split_axis=1, concat_axi...  46.8 us
    all_to_all x1, waiting for transfers between devices, local(): lax.all_to_all(send_grad, 'expert', split_axis=1, concat_axis=1, tiled=True)  45 us
    gather x1, local copies, waits for them, and re-layouts, local(): jnp.take(back_flat, position, axis=0)  11.8 us
    dot_general x2, matrix products, weight_terms(): lax.dot_general(rows_in, grad_pre, (((0,), (0,)), ((), ())), preferred_el...  7.37 us
  transfers between devices with their start and end apart: 7, of which 4 were waited for; matrix products, arithmetic and copies ran while one was open for 24% of the time, Pallas kernels for 0%

commit v1 on v0

--- a/solution.py
+++ b/solution.py
@@ -2,6 +2,7 @@
 import jax.numpy as jnp
 from jax import lax
 from jax.sharding import PartitionSpec as P
+from jax.lax import all_to_all, axis_size
 
 
 def expert_backward(rows_in, rows_grad, weight, gate_up, down):
@@ -100,9 +101,18 @@
     ).reshape(exp_local, groups, capacity)
     gate_up_terms = []
     down_terms = []
+    unite_flows = lambda array_here, which_dim, join_dim: jnp.concatenate(
+        all_to_all(
+            jnp.stack(jnp.split(array_here, axis_size("expert"), axis=which_dim)),
+            axis_name="expert",
+            split_axis=0,
+            concat_axis=0,
+        ),
+        axis=join_dim,
+    )
     arrived_in, arrived_grad, arrived_weight = (
         lax.all_to_all(send_in, "expert", split_axis=1, concat_axis=1, tiled=True),
-        lax.all_to_all(send_grad, "expert", split_axis=1, concat_axis=1, tiled=True),
+        unite_flows(send_grad, 1, 1),
         lax.all_to_all(send_weight, "expert", split_axis=1, concat_axis=1, tiled=True),
     )
     inputs_list = []

time: 365 us -> 374 us (1.025)
  waiting for transfers between devices: 206 us -> 211 us
  local copies, waits for them, and re-layouts: 68.2 us -> 72.6 us
    reshape x1 -> x0, local copies, waits for them, and re-layouts: 5.18 us -> none  [local(): jnp.take(out_grad, token_of, axis=0, mode='fill', fill_value=0)]
    all_to_all x1, waiting for transfers between devices: 45 us -> 49.5 us  [local(): all_to_all(jnp.stack(jnp.split(array_here, axis_size('expert'), axis=whic...]
    unnamed x33 -> x46, local copies, waits for them, and re-layouts: 5.39 us -> 9.93 us
  transfers between devices with their start and end apart: 7 -> 7, of which waited for: 4 -> 4; matrix products, arithmetic and copies ran while one was open for 24% -> 23% of each run, Pallas kernels for 0% -> 0%
where the time goes in v1:
time: 374 us
  waiting for transfers between devices  211 us (56%)
  local copies, waits for them, and re-layouts  72.6 us (19%)
  matrix products  28.2 us (8%)
  other arithmetic  24 us (6%)
  starting transfers between devices  23 us (6%)
  between operations  14.5 us (4%)
    reduce_scatter x1, waiting for transfers between devices, local(): lax.psum_scatter(jnp.stack(gate_up_terms).astype(jnp.bfloat16), 'dp', sca...  65.1 us
    all_to_all x1, waiting for transfers between devices, local(): lax.all_to_all(send_in, 'expert', split_axis=1, concat_axis=1, tiled=True)  50 us
    all_to_all x1, waiting for transfers between devices, local(): all_to_all(jnp.stack(jnp.split(array_here, axis_size('expert'), axis=whic...  49.5 us
    all_to_all x1, waiting for transfers between devices, local(): lax.all_to_all(jnp.stack(inputs_list), 'expert', split_axis=1, concat_axi...  46.8 us
    gather x1, local copies, waits for them, and re-layouts, local(): jnp.take(back_flat, position, axis=0)  11.8 us
    unnamed x46, local copies, waits for them, and re-layouts  9.93 us
    dot_general x2, matrix products, expert_backward(): pre_act = jnp.dot(rows_in, gate_up, preferred_element_type=jnp.float32)  7.63 us
  transfers between devices with their start and end apart: 7, of which 4 were waited for; matrix products, arithmetic and copies ran while one was open for 23% of the time, Pallas kernels for 0%

profile of v1, /device:TPU:0, one launch (start us, length us, event | category | flops | bytes accessed | tf_op | source)
XLA Modules:
  0.0 373.7 jit_solution(11588539590754484071)
XLA Ops:
  7.2 0.8 copy.52
  8.7 4.3 %scatter_custom_fusion = s32[1152]{0:T(1024)S(1)} fusion(s32[1024]{0:T(1024)S(1)} %bitcast.137, s32[1024]{0:T(1024)S(1)} %iota.30, s32[]{:T(128)} %constant.102.clone.1), kind=kCustom, calls=%fused_computation.135 | custom fusion | bytes 4612 | tf_op jit(solution)/shard_map/scatter | solution.py:91
  13.0 0.8 copy.58
  14.0 7.3 %gather_fusion = bf16[1152]{0:T(1024)(128)(2,1)S(1)} fusion(bf16[1024]{0:T(1024)(128)(2,1)S(1)} %reshape.252, s32[2048]{0:T(1024)S(1)} %get-tuple-element.42), kind=kCustom, calls=%fused_computation.2 | custom fusion | bytes 9216 | tf_op jit(solution)/shard_map/jit(_take)/gather | solution.py:99
  22.0 5.2 %all-to-all-start = ((bf16[2,8,72]{2,0,1:T(2,128)(2,1)}), bf16[2,8,72]{2,0,1:T(2,128)(2,1)S(1)}, u32[]{:S(2)}, u32[]{:S(2)}) async-start(bf16[2,8,72]{2,0,1:T(2,128)(2,1)} %copy.59), calls=%async_computation | async-start | bytes 8192 | tf_op jit(solution)/shard_map/all_to_all | solution.py:116
  27.1 5.9 %gather_fusion.3 = bf16[1152,2048]{1,0:T(8,128)(2,1)} fusion(bf16[128,2048]{1,0:T(8,128)(2,1)S(1)} %copy-done, s32[2048]{0:T(1024)S(1)} %get-tuple-element.41), kind=kCustom, calls=%fused_computation.clone | custom fusion | bytes 9441792 | tf_op jit(solution)/shard_map/jit(_take)/gather | solution.py:96
  33.1 5.9 %gather_fusion.4 = bf16[1152,2048]{1,0:T(8,128)(2,1)} fusion(bf16[128,2048]{1,0:T(8,128)(2,1)S(1)} %copy-done.2, s32[2048]{0:T(1024)S(1)} %get-tuple-element.41), kind=kCustom, calls=%fused_computation.1.clone | custom fusion | bytes 9441792 | tf_op jit(solution)/shard_map/jit(_take)/gather | solution.py:93
  39.0 5.7 %broadcast_select_fusion = (bf16[1152,2048]{1,0:T(8,128)(2,1)}, bf16[1152,2048]{1,0:T(8,128)(2,1)S(1)}) fusion(bf16[1152,2048]{1,0:T(8,128)(2,1)} %gather_fusion.4, pred[1152]{0:T(1024)(128)(4,1)S(1)} %get-tuple-element.25, bf16[1152,2048]{1,0:T(8,128)(2,1)} %gather_fusion.3), kind=kLoop, calls=%fused_computation.8 | loop fusion | flops 4718592 | bytes 18875520 | tf_op jit(solution)/shard_map/jit(_take)/select_n | solution.py:93
  44.7 0.9 fusion.45
  45.6 0.9 fusion.44
  46.5 0.9 fusion.43
  47.4 0.9 fusion.42
  48.2 0.9 fusion.41
  49.1 0.9 fusion.40
  50.0 0.9 fusion.39
  50.8 0.9 fusion.38
  51.7 4.6 %all-to-all-start.1 = ((bf16[8,2,1,72,2048]{4,3,1,2,0:T(8,128)(2,1)}), bf16[8,2,1,72,2048]{4,3,1,2,0:T(8,128)(2,1)}, u32[]{:S(2)}, u32[]{:S(2)}) async-start(bf16[8,2,1,72,2048]{4,3,1,2,0:T(8,128)(2,1)} %fusion.38), calls=%async_computation.1 | async-start | bytes 9437184 | tf_op jit(solution)/shard_map/all_to_all | solution.py:105
  56.4 5.2 %copy.67 = bf16[2,8,72,2048]{3,2,0,1:T(8,128)(2,1)} copy(bf16[2,8,72,2048]{3,2,1,0:T(8,128)(2,1)} %bitcast.117) | data formatting | bytes 9437184 | tf_op jit(solution)/shard_map/reshape | solution.py:93
  61.6 49.5 %all-to-all-done.1 = bf16[8,2,1,72,2048]{4,3,1,2,0:T(8,128)(2,1)} async-done(((bf16[8,2,1,72,2048]{4,3,1,2,0:T(8,128)(2,1)}), bf16[8,2,1,72,2048]{4,3,1,2,0:T(8,128)(2,1)}, u32[]{:S(2)}, u32[]{:S(2)}) %all-to-all-start.1) | async-done | bytes 4718624 | tf_op jit(solution)/shard_map/all_to_all | solution.py:105
  111.1 4.6 %all-to-all-start.2 = ((bf16[2,8,72,2048]{3,2,0,1:T(8,128)(2,1)}), bf16[2,8,72,2048]{3,2,0,1:T(8,128)(2,1)}, u32[]{:S(2)}, u32[]{:S(2)}) async-start(bf16[2,8,72,2048]{3,2,0,1:T(8,128)(2,1)} %copy.67), calls=%async_computation.2 | async-start | bytes 9437184 | tf_op jit(solution)/shard_map/all_to_all | solution.py:114
  116.1 4.3 %fusion.77 = (bf16[1,8,1,72,2048]{4,3,0,2,1:T(8,128)(2,1)}, bf16[1,8,1,72,2048]{4,3,0,2,1:T(8,128)(2,1)S(1)}) fusion(bf16[2,8,1,72,2048]{4,3,0,2,1:T(8,128)(2,1)} %bitcast.13), kind=kLoop, calls=%fused_computation.145 | loop fusion | bytes 9437184 | tf_op jit(solution)/shard_map/slice | solution.py:124
  120.5 50.0 %all-to-all-done.2 = bf16[2,8,72,2048]{3,2,0,1:T(8,128)(2,1)} async-done(((bf16[2,8,72,2048]{3,2,0,1:T(8,128)(2,1)}), bf16[2,8,72,2048]{3,2,0,1:T(8,128)(2,1)}, u32[]{:S(2)}, u32[]{:S(2)}) %all-to-all-start.2) | async-done | bytes 4718624 | tf_op jit(solution)/shard_map/all_to_all | solution.py:114
  170.5 2.8 fusion.76
  173.3 5.6 %fusion.7 = f32[576,768]{1,0:T(8,128)S(1)} fusion(bf16[576,2048]{1,0:T(8,128)(2,1)S(1)} %bitcast.132, bf16[2,2048,768]{2,1,0:T(8,128)(2,1)} %param.12), kind=kOutput, calls=%fused_computation.21 | convolution fusion | flops 1811939328 | bytes 7274496 | tf_op jit(solution)/shard_map/dot_general | solution.py:9
  178.9 2.5 fusion.32
  181.5 1.5 fusion.21
  183.0 2.0 fusion.3
  185.0 2.7 fusion.34
  187.7 1.5 fusion.22
  189.2 1.9 pad_maximum_fusion.2
  191.4 1.4 copy-done.7
  192.9 2.9 fusion.15
  195.8 2.9 fusion.16
  198.7 3.2 pad_maximum_fusion
  202.7 3.3 all-to-all-start.4
  206.0 4.2 %fusion.9 = bf16[576,2048]{1,0:T(8,128)(2,1)S(1)} fusion(bf16[2,2048,768]{2,1,0:T(8,128)(2,1)} %param.12, bf16[576,384]{1,0:T(8,128)(2,1)S(1)} %get-tuple-element.35, bf16[576,384]{1,0:T(8,128)(2,1)} %get-tuple-element.36), kind=kOutput, calls=%fused_computation.24 | convolution fusion | flops 1814888448 | bytes 6389760 | tf_op jit(solution)/shard_map/dot_general | solution.py:25
  210.3 2.0 fusion.12
  212.4 2.6 pad_maximum_fusion.1
  215.0 4.9 %all-to-all-start.3 = ((bf16[2,8,72,2048]{3,2,0,1:T(8,128)(2,1)}), bf16[2,8,72,2048]{3,2,0,1:T(8,128)(2,1)}, u32[]{:S(2)}, u32[]{:S(2)}) async-start(bf16[2,8,72,2048]{3,2,0,1:T(8,128)(2,1)} %pad_maximum_fusion.1), calls=%async_computation.3 | async-start | bytes 9437184 | tf_op jit(solution)/shard_map/all_to_all | solution.py:133
  220.1 6.8 %gather_fusion.2 = bf16[1024]{0:T(1024)(128)(2,1)S(1)} fusion(bf16[1152]{0:T(1024)(128)(2,1)S(1)} %reshape.257, s32[1024]{0:T(1024)S(1)} %broadcast_clamp_fusion), kind=kCustom, calls=%fused_computation.4 | custom fusion | bytes 8192 | tf_op jit(solution)/shard_map/jit(_take)/gather | solution.py:155
  227.1 0.7 copy.73
  227.7 46.8 %all-to-all-done.3 = bf16[2,8,72,2048]{3,2,0,1:T(8,128)(2,1)} async-done(((bf16[2,8,72,2048]{3,2,0,1:T(8,128)(2,1)}), bf16[2,8,72,2048]{3,2,0,1:T(8,128)(2,1)}, u32[]{:S(2)}, u32[]{:S(2)}) %all-to-all-start.3) | async-done | bytes 4718624 | tf_op jit(solution)/shard_map/all_to_all | solution.py:133
  274.6 5.3 %copy.70 = bf16[2,8,72,2048]{3,2,1,0:T(8,128)(2,1)} copy(bf16[2,8,72,2048]{3,2,0,1:T(8,128)(2,1)} %all-to-all-done.3) | data formatting | bytes 9437184 | tf_op jit(solution)/shard_map/all_to_all | solution.py:133
  279.8 11.8 %gather_fusion.1 = bf16[1024,2048]{1,0:T(8,128)(2,1)} fusion(bf16[1152,2048]{1,0:T(8,128)(2,1)} %bitcast.116, s32[1024]{0:T(1024)S(1)} %broadcast_clamp_fusion), kind=kCustom, calls=%fused_computation.3 | custom fusion | bytes 8392704 | tf_op jit(solution)/shard_map/jit(_take)/gather | solution.py:153
  291.6 5.2 %fusion = bf16[128,2048]{1,0:T(8,128)(2,1)} fusion(bf16[1024,2048]{1,0:T(8,128)(2,1)} %gather_fusion.1, pred[128,8]{1,0:T(8,128)(4,1)S(1)} %get-tuple-element.20), kind=kLoop, calls=%fused_computation.11 | loop fusion | flops 3932160 | bytes 4719616 | tf_op jit(solution)/shard_map/reduce_sum | solution.py:154
  296.8 2.2 multiply_convert_fusion.1
  299.0 65.1 %reduce-scatter.3.cloned.1.call-done = bf16[2,512,768]{2,1,0:T(8,128)(2,1)} async-done(((bf16[2,2048,768]{2,1,0:T(8,128)(2,1)}), bf16[2,512,768]{2,1,0:T(8,128)(2,1)}) %reduce-scatter.3.cloned.1.call-update) | async-done | bytes 1572880 | tf_op jit(solution)/shard_map/reduce_scatter | solution.py:141
  364.1 2.8 multiply_convert_fusion
  (72 shorter events, 3.5 us)
Async XLA Ops:
  7.2 20.0 %copy-start = (bf16[128,2048]{1,0:T(8,128)(2,1)S(1)}, bf16[128,2048]{1,0:T(8,128)(2,1)}, u32[]{:S(2)}) copy-start(bf16[128,2048]{1,0:T(8,128)(2,1)} %param.9) | copy-start | bytes 1572868
  22.0 29.8 %all-to-all-start = ((bf16[2,8,72]{2,0,1:T(2,128)(2,1)}), bf16[2,8,72]{2,0,1:T(2,128)(2,1)S(1)}, u32[]{:S(2)}, u32[]{:S(2)}) async-start(bf16[2,8,72]{2,0,1:T(2,128)(2,1)} %copy.59), calls=%async_computation | async-start | bytes 8192 | tf_op jit(solution)/shard_map/all_to_all | solution.py:116
  27.1 5.9 %copy-start.2 = (bf16[128,2048]{1,0:T(8,128)(2,1)S(1)}, bf16[128,2048]{1,0:T(8,128)(2,1)}, u32[]{:S(2)}) copy-start(bf16[128,2048]{1,0:T(8,128)(2,1)} %param.8) | copy-start | bytes 1572868
  51.7 59.4 %all-to-all-start.1 = ((bf16[8,2,1,72,2048]{4,3,1,2,0:T(8,128)(2,1)}), bf16[8,2,1,72,2048]{4,3,1,2,0:T(8,128)(2,1)}, u32[]{:S(2)}, u32[]{:S(2)}) async-start(bf16[8,2,1,72,2048]{4,3,1,2,0:T(8,128)(2,1)} %fusion.38), calls=%async_computation.1 | async-start | bytes 9437184 | tf_op jit(solution)/shard_map/all_to_all | solution.py:105
  111.1 59.4 %all-to-all-start.2 = ((bf16[2,8,72,2048]{3,2,0,1:T(8,128)(2,1)}), bf16[2,8,72,2048]{3,2,0,1:T(8,128)(2,1)}, u32[]{:S(2)}, u32[]{:S(2)}) async-start(bf16[2,8,72,2048]{3,2,0,1:T(8,128)(2,1)} %copy.67), calls=%async_computation.2 | async-start | bytes 9437184 | tf_op jit(solution)/shard_map/all_to_all | solution.py:114
  115.7 181.1 %reduce-scatter.5.cloned.1.call-start = ((), (), s32[]{:S(2)}) async-start(), calls=%async_computation.8 | async-start | bytes 3932160 | tf_op jit(solution)/shard_map/reduce_scatter | solution.py:144
  173.2 5.7 %copy-start.6 = (bf16[1,8,72,2048]{3,2,0,1:T(8,128)(2,1)}, bf16[1,8,72,2048]{3,2,0,1:T(8,128)(2,1)S(1)}, u32[]{:S(2)}) copy-start(bf16[1,8,72,2048]{3,2,0,1:T(8,128)(2,1)S(1)} %get-tuple-element.27) | copy-start | bytes 7077892
  173.2 9.8 %copy-start.4 = (bf16[1,8,72,2048]{3,2,0,1:T(8,128)(2,1)}, bf16[1,8,72,2048]{3,2,0,1:T(8,128)(2,1)S(1)}, u32[]{:S(2)}) copy-start(bf16[1,8,72,2048]{3,2,0,1:T(8,128)(2,1)S(1)} %get-tuple-element.28) | copy-start | bytes 7077892
  173.2 5.7 %copy-start.3 = (bf16[1,8,1,72,2048]{4,3,0,2,1:T(8,128)(2,1)S(1)}, bf16[1,8,1,72,2048]{4,3,0,2,1:T(8,128)(2,1)}, u32[]{:S(2)}) copy-start(bf16[1,8,1,72,2048]{4,3,0,2,1:T(8,128)(2,1)} %get-tuple-element.29) | copy-start | bytes 7077892
  173.2 5.7 %copy-start.8 = (bf16[2,384,2048]{2,1,0:T(8,128)(2,1)S(1)}, bf16[2,384,2048]{2,1,0:T(8,128)(2,1)}, u32[]{:S(2)}) copy-start(bf16[2,384,2048]{2,1,0:T(8,128)(2,1)} %param.13) | copy-start | bytes 9437188
  173.2 9.7 %slice-start = ((s8[6291456]{0:T(1024)(128)(4,1)}), s8[2097152]{0:T(1024)(128)(4,1)S(1)}, s32[]{:S(2)}) async-start(s8[6291456]{0:T(1024)(128)(4,1)} %bitcast.139), calls=%async_computation.9 | async-start | bytes 4194304
  178.9 4.1 %slice-start.1 = ((s8[6291456]{0:T(1024)(128)(4,1)}), s8[4194304]{0:T(1024)(128)(4,1)S(1)}, s32[]{:S(2)}) async-start(s8[6291456]{0:T(1024)(128)(4,1)} %bitcast.139), calls=%async_computation.10 | async-start | bytes 8388608
  191.1 1.7 copy-start.7
  191.1 1.7 copy-start.9
  191.2 172.9 %reduce-scatter.3.cloned.1.call-start = ((), (), s32[]{:S(2)}) async-start(), calls=%async_computation.7 | async-start | bytes 7864320 | tf_op jit(solution)/shard_map/reduce_scatter | solution.py:141
  192.9 2.9 copy-start.5
  192.9 2.9 copy-start.10
  192.9 2.9 copy-start.12
  201.9 8.3 %slice-start.2 = ((s8[6291456]{0:T(1024)(128)(4,1)}), s8[2097152]{0:T(1024)(128)(4,1)S(1)}, s32[]{:S(2)}) async-start(s8[6291456]{0:T(1024)(128)(4,1)} %bitcast.141), calls=%async_computation.11 | async-start | bytes 4194304
  202.7 12.3 %all-to-all-start.4 = ((bf16[2,8,72]{2,0,1:T(2,128)(2,1)}), bf16[2,8,72]{2,0,1:T(2,128)(2,1)S(1)}, u32[]{:S(2)}, u32[]{:S(2)}) async-start(bf16[2,8,72]{2,0,1:T(2,128)(2,1)} %copy.71), calls=%async_computation.4 | async-start | bytes 8192 | tf_op jit(solution)/shard_map/all_to_all | solution.py:134
  206.0 4.3 %slice-start.3 = ((s8[6291456]{0:T(1024)(128)(4,1)}), s8[4194304]{0:T(1024)(128)(4,1)S(1)}, s32[]{:S(2)}) async-start(s8[6291456]{0:T(1024)(128)(4,1)} %bitcast.141), calls=%async_computation.12 | async-start | bytes 8388608
  206.0 4.3 %copy-start.11 = (bf16[576,384]{1,0:T(8,128)(2,1)S(1)}, bf16[576,384]{1,0:T(8,128)(2,1)}, u32[]{:S(2)}) copy-start(bf16[576,384]{1,0:T(8,128)(2,1)} %get-tuple-element.37) | copy-start | bytes 1327108
  206.0 4.3 %copy-start.13 = (bf16[576,384]{1,0:T(8,128)(2,1)S(1)}, bf16[576,384]{1,0:T(8,128)(2,1)}, u32[]{:S(2)}) copy-start(bf16[576,384]{1,0:T(8,128)(2,1)} %get-tuple-element.38) | copy-start | bytes 1327108
  215.0 59.6 %all-to-all-start.3 = ((bf16[2,8,72,2048]{3,2,0,1:T(8,128)(2,1)}), bf16[2,8,72,2048]{3,2,0,1:T(8,128)(2,1)}, u32[]{:S(2)}, u32[]{:S(2)}) async-start(bf16[2,8,72,2048]{3,2,0,1:T(8,128)(2,1)} %pad_maximum_fusion.1), calls=%async_computation.3 | async-start | bytes 9437184 | tf_op jit(solution)/shard_map/all_to_all | solution.py:133
  291.6 75.3 %copy-start.1 = (bf16[128,2048]{1,0:T(8,128)(2,1)S(1)}, bf16[128,2048]{1,0:T(8,128)(2,1)}, u32[]{:S(2)}) copy-start(bf16[128,2048]{1,0:T(8,128)(2,1)} %param.9) | copy-start | bytes 1572868
Sparse Core Ops, SparseCore 0:
  191.3 59.6 reduce-scatter.4
  253.3 110.7 reduce-scatter.2
